TPU v7x, 32 devices: a whole 2x2x4 slice. The times are simulated.
32 devices in a mesh: sec: 4 (over y, x), tile: 8 (over z, core).
Axes of the slice: x: 2, y: 2, z: 4, core: 2. Of those that a mesh axis runs over, the one named last changes fastest.
Arguments:
- displacement: float32 [2, 16, 256, 256], P(None, 'sec', 'tile'), may hold values from -3 to 3
- coupling: float32 [4, 16, 256, 256], P(None, 'sec', 'tile'), may hold values from 0.1 to 1
- matches: float32 [4, 2, 16, 256, 256], P(None, None, 'sec', 'tile'), may hold values from -3 to 3
- step_sizes: float32 [2, 8], replicated, may hold values from 0.1 to 0.35
- restarts: int32 [2, 8], replicated, may hold values 0 or 1
- images: float32 [4, 64, 256, 256], P('sec', 'tile'), may hold values from 0 to 1
- block_anchor: int32 [4, 64], P('sec', 'tile'), may hold values from 0 to 32767
- block_dest: int32 [4, 64, 1], P('sec', 'tile'), may hold values from 0 to 7; in each aligned block of 8 rows (0 to 7, 8 to 15, ..., all dimensions but the last counted through in order) at most 2 rows name the same one
- block_slot: int32 [4, 64], P('sec', 'tile'), may hold values from 0 to 1
- block_offset: int32 [4, 64, 2], P('sec', 'tile'), may hold values from 0 to 128
- block_count: int32 [4, 8], P('sec', 'tile'), may hold values from 6 to 8, as said below
Outputs:
- aligned: float32 [2, 16, 256, 256], P(None, 'sec', 'tile')
- spans: float32 [64, 384, 384], P(('sec', 'tile'))
Inputs may be any that keep to these rules, and one draw needn't show every extreme that they name: `block_dest`: no tile index is named by more than 2 of the block slots of one device, and 2 is reached. `block_count`: some device uses all 8 slots.
All inputs are finite; a program needn't handle non-finite values.
Results may differ from a plain program's by a relative error of at most 0.0003.
Values sent between devices are 32-bit elements; how exact they have to be, the bound alone decides.
A program may use at most 128 MiB of HBM per device.

v0:
```python
import jax
import jax.numpy as jnp
from jax import lax
from jax.sharding import PartitionSpec as P

OUTER = 2
FIRE_STEPS = 8
BPP = 256
CH = 384
SPAN_DEV = 2
STIFFNESS = 1.0
MIXING = 0.1
EPSILON = 1e-06
SPEED_CAP = 0.1
PRECISE = lax.Precision.HIGHEST


def with_halo(array, sides, width):
    for axis, dim in sides:
        size, length = (lax.axis_size(axis), array.shape[dim])
        up = [(i, (i + 1) % size) for i in range(size - 1)]
        down = [(j, i) for i, j in up]
        last = lax.slice_in_dim(array, length - width, length, axis=dim)
        leading = lax.slice_in_dim(array, 0, width, axis=dim)
        before = lax.ppermute(last, axis, up)
        after = lax.ppermute(leading, axis, down)
        array = jnp.concatenate([before, array, after], axis=dim)
    return array


def forces(current, refer, coupling, matches, first_sec, sections_all):
    strain = current - refer
    rimmed = with_halo(strain, (("tile", 2),), 1)
    sides = jnp.pad(strain, ((0, 0), (0, 0), (0, 0), (1, 1)))
    summed = STIFFNESS * (
        rimmed[:, :, 2:] + rimmed[:, :, :-2] + sides[..., 2:] + sides[..., :-2] - 4.0 * strain
    )
    stacked = with_halo(current, (("sec", 1),), 2)
    sections_dev = current.shape[1]
    section = first_sec + jnp.arange(sections_dev)
    for which_k, reach in enumerate((-2, -1, 1, 2)):
        beside = stacked[:, 2 + reach : 2 + reach + sections_dev]
        usable = ((section + reach >= 0) & (section + reach < sections_all)).astype(jnp.float32)
        summed = summed + usable[None, :, None, None] * coupling[which_k][None] * (
            beside + matches[which_k] - current
        )
    return summed


def hat_rows(shift, size, source):
    row_pos = jnp.arange(size).astype(jnp.float32)[None, :, None]
    src_pos = jnp.arange(source).astype(jnp.float32)[None, None, :]
    return jnp.maximum(0.0, 1.0 - jnp.abs(row_pos - src_pos - shift[:, None, None]))


def warp_blocks(blocks_in, shift_y, shift_x):
    row_hats = hat_rows(shift_y, CH, BPP)
    col_hats = hat_rows(shift_x, CH, BPP)
    halfway = jnp.einsum("bij,bkj->bik", blocks_in, col_hats, precision=PRECISE)
    return jnp.einsum("bri,bik->brk", row_hats, halfway, precision=PRECISE)


def body(
    displacement,
    coupling,
    matches,
    step_sizes,
    restarts,
    images,
    block_anchor,
    block_dest,
    block_slot,
    block_offset,
    block_count,
):
    sections_dev = displacement.shape[1]
    first_sec = lax.axis_index("sec") * sections_dev
    sections_all = sections_dev * lax.axis_size("sec")
    node_total = 2.0 * sections_all * displacement.shape[3] * displacement.shape[3]
    current = displacement
    refer = displacement
    velocity = jnp.zeros_like(displacement)
    for outer_step in range(OUTER):
        for inner_step in range(FIRE_STEPS):
            delta = step_sizes[outer_step, inner_step]
            push = forces(current, refer, coupling, matches, first_sec, sections_all)
            velocity = velocity + delta * push
            speed_sq, push_sq = lax.psum(
                (jnp.sum(velocity * velocity), jnp.sum(push * push)), ("sec", "tile")
            )
            ratio = jnp.sqrt(speed_sq + EPSILON) / jnp.sqrt(push_sq + EPSILON)
            limit = jnp.minimum(1.0, SPEED_CAP / jnp.sqrt(speed_sq / node_total + EPSILON))
            retain = 1.0 - restarts[outer_step, inner_step].astype(jnp.float32)
            velocity = limit * retain * ((1.0 - MIXING) * velocity + MIXING * ratio * push)
            current = current + delta * velocity
        refer = current
        velocity = jnp.zeros_like(current)
    flat_disp = current.reshape(2, -1)
    moved = jnp.take(flat_disp, block_anchor[0], axis=1)
    blocks_here = block_anchor.shape[1]
    usable = (jnp.arange(blocks_here) < block_count[0, 0]).astype(jnp.float32)
    offsets = block_offset[0].astype(jnp.float32)
    shift_y = offsets[:, 0] + moved[0]
    shift_x = offsets[:, 1] + moved[1]
    owners = block_dest[0, :, 0]
    slot_hot = (block_slot[0][:, None] == jnp.arange(SPAN_DEV)[None, :]).astype(
        jnp.float32
    ) * usable[:, None]
    tiles = lax.axis_size("tile")
    capacity = max(2, 2 * blocks_here // tiles)
    owner_hot = (owners[:, None] == jnp.arange(tiles)[None, :]).astype(jnp.int32)
    rank_all = jnp.cumsum(owner_hot, axis=0) - owner_hot
    rank_own = jnp.sum(rank_all * owner_hot, axis=1)
    position = owners * capacity + rank_own
    placer = (position[None, :] == jnp.arange(tiles * capacity)[:, None]).astype(jnp.float32)
    send_blocks = jnp.einsum("sb,bij->sij", placer, images[0], precision=PRECISE).reshape(
        tiles, capacity, BPP, BPP
    )
    shifts_both = jnp.stack([shift_y, shift_x], axis=1)
    send_shift = jnp.dot(placer, shifts_both, precision=PRECISE).reshape(tiles, capacity, 2)
    send_select = jnp.dot(placer, slot_hot, precision=PRECISE).reshape(tiles, capacity, SPAN_DEV)
    blocks_in = lax.all_to_all(send_blocks, "tile", split_axis=0, concat_axis=0, tiled=True)
    shift_in = lax.all_to_all(send_shift, "tile", split_axis=0, concat_axis=0, tiled=True)
    select_in = lax.all_to_all(send_select, "tile", split_axis=0, concat_axis=0, tiled=True)
    sources = blocks_in.shape[0]
    items = blocks_in.shape[1]
    drawn = warp_blocks(
        blocks_in.reshape(sources * items, BPP, BPP),
        shift_in[..., 0].reshape(-1),
        shift_in[..., 1].reshape(-1),
    )
    drawn = drawn.reshape(sources, items, CH, CH)
    pieces = jnp.einsum("skc,skrq->kcrq", select_in, drawn, precision=PRECISE)
    spans = jnp.sum(pieces, axis=0)
    return (current, spans)


def solution(mesh):
    placed = (
        P(None, "sec", "tile", None),
        P(None, "sec", "tile", None),
        P(None, None, "sec", "tile", None),
        P(),
        P(),
        P("sec", "tile", None, None),
        P("sec", "tile"),
        P("sec", "tile", None),
        P("sec", "tile"),
        P("sec", "tile", None),
        P("sec", "tile"),
    )
    return jax.shard_map(
        body,
        mesh=mesh,
        in_specs=placed,
        out_specs=(P(None, "sec", "tile", None), P(("sec", "tile"), None, None)),
        check_vma=False,
    )
```

profile of v0, /device:TPU:0, one launch (start us, length us, event | category | flops | bytes accessed | tf_op | source)
XLA Modules:
  0.0 1109.9 jit_solution(523799049433969451)
XLA Ops:
  1.8 4.9 collective-permute-start.2
  16.2 3.0 collective-permute-start.1
  23.0 43.6 %all-reduce.31 = (f32[]{:T(128)}, f32[]{:T(128)}) all-reduce(f32[]{:T(128)} %get-tuple-element.41, f32[]{:T(128)} %get-tuple-element.40), channel_id=1, replica_groups=mesh['sec'=4,'tile'=8] {'sec','tile'}, use_global_device_ids=true, to_apply=%region_1.2 | all-reduce | flops 2 | bytes 16 | tf_op jit(solution)/shard_map/psum | solution.py:88
  69.4 4.2 collective-permute-start.6
  83.4 42.6 %all-reduce.30 = (f32[]{:T(128)}, f32[]{:T(128)}) all-reduce(f32[]{:T(128)} %get-tuple-element.39, f32[]{:T(128)} %get-tuple-element.38), channel_id=1, replica_groups=mesh['sec'=4,'tile'=8] {'sec','tile'}, use_global_device_ids=true, to_apply=%region_5.6 | all-reduce | flops 2 | bytes 16 | tf_op jit(solution)/shard_map/psum | solution.py:88
  129.3 4.2 collective-permute-start.10
  136.2 3.0 collective-permute-start.9
  142.7 41.5 %all-reduce.29 = (f32[]{:T(128)}, f32[]{:T(128)}) all-reduce(f32[]{:T(128)} %get-tuple-element.37, f32[]{:T(128)} %get-tuple-element.36), channel_id=1, replica_groups=mesh['sec'=4,'tile'=8] {'sec','tile'}, use_global_device_ids=true, to_apply=%region_9.10 | all-reduce | flops 2 | bytes 16 | tf_op jit(solution)/shard_map/psum | solution.py:88
  187.1 4.2 collective-permute-start.14
  193.9 3.0 collective-permute-start.13
  200.4 42.6 %all-reduce.28 = (f32[]{:T(128)}, f32[]{:T(128)}) all-reduce(f32[]{:T(128)} %get-tuple-element.35, f32[]{:T(128)} %get-tuple-element.34), channel_id=1, replica_groups=mesh['sec'=4,'tile'=8] {'sec','tile'}, use_global_device_ids=true, to_apply=%region_13.14 | all-reduce | flops 2 | bytes 16 | tf_op jit(solution)/shard_map/psum | solution.py:88
  245.7 4.2 collective-permute-start.18
  259.0 41.5 %all-reduce.27 = (f32[]{:T(128)}, f32[]{:T(128)}) all-reduce(f32[]{:T(128)} %get-tuple-element.33, f32[]{:T(128)} %get-tuple-element.32), channel_id=1, replica_groups=mesh['sec'=4,'tile'=8] {'sec','tile'}, use_global_device_ids=true, to_apply=%region_17.18 | all-reduce | flops 2 | bytes 16 | tf_op jit(solution)/shard_map/psum | solution.py:88
  303.4 4.2 collective-permute-start.22
  310.3 3.0 collective-permute-start.21
  316.8 42.6 %all-reduce.26 = (f32[]{:T(128)}, f32[]{:T(128)}) all-reduce(f32[]{:T(128)} %get-tuple-element.31, f32[]{:T(128)} %get-tuple-element.30), channel_id=1, replica_groups=mesh['sec'=4,'tile'=8] {'sec','tile'}, use_global_device_ids=true, to_apply=%region_21.22 | all-reduce | flops 2 | bytes 16 | tf_op jit(solution)/shard_map/psum | solution.py:88
  362.2 4.2 collective-permute-start.26
  375.4 41.5 %all-reduce.25 = (f32[]{:T(128)}, f32[]{:T(128)}) all-reduce(f32[]{:T(128)} %get-tuple-element.29, f32[]{:T(128)} %get-tuple-element.28), channel_id=1, replica_groups=mesh['sec'=4,'tile'=8] {'sec','tile'}, use_global_device_ids=true, to_apply=%region_25.26 | all-reduce | flops 2 | bytes 16 | tf_op jit(solution)/shard_map/psum | solution.py:88
  419.6 4.2 collective-permute-start.30
  426.4 3.2 collective-permute-start.29
  433.0 42.6 %all-reduce.24 = (f32[]{:T(128)}, f32[]{:T(128)}) all-reduce(f32[]{:T(128)} %get-tuple-element.27, f32[]{:T(128)} %get-tuple-element.26), channel_id=1, replica_groups=mesh['sec'=4,'tile'=8] {'sec','tile'}, use_global_device_ids=true, to_apply=%region_29.30 | all-reduce | flops 2 | bytes 16 | tf_op jit(solution)/shard_map/psum | solution.py:88
  478.4 4.2 collective-permute-start.34
  491.6 41.4 %all-reduce.23 = (f32[]{:T(128)}, f32[]{:T(128)}) all-reduce(f32[]{:T(128)} %get-tuple-element.25, f32[]{:T(128)} %get-tuple-element.24), channel_id=1, replica_groups=mesh['sec'=4,'tile'=8] {'sec','tile'}, use_global_device_ids=true, to_apply=%region_33.34 | all-reduce | flops 2 | bytes 16 | tf_op jit(solution)/shard_map/psum | solution.py:88
  535.7 4.2 collective-permute-start.38
  549.6 42.6 %all-reduce.22 = (f32[]{:T(128)}, f32[]{:T(128)}) all-reduce(f32[]{:T(128)} %get-tuple-element.23, f32[]{:T(128)} %get-tuple-element.22), channel_id=1, replica_groups=mesh['sec'=4,'tile'=8] {'sec','tile'}, use_global_device_ids=true, to_apply=%region_37.38 | all-reduce | flops 2 | bytes 16 | tf_op jit(solution)/shard_map/psum | solution.py:88
  595.8 4.2 collective-permute-start.42
  606.5 3.5 all-to-all-start
  612.3 42.3 %all-reduce.21 = (f32[]{:T(128)}, f32[]{:T(128)}) all-reduce(f32[]{:T(128)} %get-tuple-element.21, f32[]{:T(128)} %get-tuple-element.20), channel_id=1, replica_groups=mesh['sec'=4,'tile'=8] {'sec','tile'}, use_global_device_ids=true, to_apply=%region_41.42 | all-reduce | flops 2 | bytes 16 | tf_op jit(solution)/shard_map/psum | solution.py:88
  657.4 4.2 collective-permute-start.46
  670.8 42.6 %all-reduce.20 = (f32[]{:T(128)}, f32[]{:T(128)}) all-reduce(f32[]{:T(128)} %get-tuple-element.19, f32[]{:T(128)} %get-tuple-element.18), channel_id=1, replica_groups=mesh['sec'=4,'tile'=8] {'sec','tile'}, use_global_device_ids=true, to_apply=%region_45.46 | all-reduce | flops 2 | bytes 16 | tf_op jit(solution)/shard_map/psum | solution.py:88
  716.0 4.2 collective-permute-start.50
  729.3 41.5 %all-reduce.19 = (f32[]{:T(128)}, f32[]{:T(128)}) all-reduce(f32[]{:T(128)} %get-tuple-element.17, f32[]{:T(128)} %get-tuple-element.16), channel_id=1, replica_groups=mesh['sec'=4,'tile'=8] {'sec','tile'}, use_global_device_ids=true, to_apply=%region_49.50 | all-reduce | flops 2 | bytes 16 | tf_op jit(solution)/shard_map/psum | solution.py:88
  773.7 4.2 collective-permute-start.54
  787.0 42.6 %all-reduce.18 = (f32[]{:T(128)}, f32[]{:T(128)}) all-reduce(f32[]{:T(128)} %get-tuple-element.15, f32[]{:T(128)} %get-tuple-element.14), channel_id=1, replica_groups=mesh['sec'=4,'tile'=8] {'sec','tile'}, use_global_device_ids=true, to_apply=%region_53.54 | all-reduce | flops 2 | bytes 16 | tf_op jit(solution)/shard_map/psum | solution.py:88
  832.4 4.2 collective-permute-start.58
  845.6 41.7 %all-reduce.17 = (f32[]{:T(128)}, f32[]{:T(128)}) all-reduce(f32[]{:T(128)} %get-tuple-element.13, f32[]{:T(128)} %get-tuple-element.12), channel_id=1, replica_groups=mesh['sec'=4,'tile'=8] {'sec','tile'}, use_global_device_ids=true, to_apply=%region_57.58 | all-reduce | flops 2 | bytes 16 | tf_op jit(solution)/shard_map/psum | solution.py:88
  890.0 4.2 collective-permute-start.62
  903.2 42.6 %all-reduce.16 = (f32[]{:T(128)}, f32[]{:T(128)}) all-reduce(f32[]{:T(128)} %get-tuple-element.11, f32[]{:T(128)} %get-tuple-element.10), channel_id=1, replica_groups=mesh['sec'=4,'tile'=8] {'sec','tile'}, use_global_device_ids=true, to_apply=%region_61.62 | all-reduce | flops 2 | bytes 16 | tf_op jit(solution)/shard_map/psum | solution.py:88
  948.4 8.5 copy.33
  957.0 6.3 gather_fusion
  964.4 3.5 all-to-all-start.1
  967.9 4.3 fusion.20
  972.3 3.3 copy.36
  975.5 5.1 all-to-all-start.2
  981.0 93.7 %all-to-all-done.2 = f32[8,2,256,256]{3,2,1,0:T(8,128)} async-done(((f32[8,2,256,256]{3,2,1,0:T(8,128)}), f32[8,2,256,256]{3,2,1,0:T(8,128)}, u32[]{:S(2)}, u32[]{:S(2)}) %all-to-all-start.2) | async-done | bytes 4194336 | tf_op jit(solution)/shard_map/all_to_all | solution.py:122
  1074.7 10.7 fusion.2
  1085.4 12.1 %fusion.7 = f32[16,384,384]{2,1,0:T(8,128)S(1)} fusion(f32[16,256,384]{2,1,0:T(8,128)S(1)} %fusion.2, f32[16]{0:T(128)S(1)} %sub.587, f32[384,256]{1,0:T(8,128)S(1)} %broadcast_subtract_fusion), kind=kOutput, calls=%fused_computation.8 | convolution fusion | flops 7254048768 | bytes 16121920 | tf_op jit(solution)/shard_map/bri,bik->brk/dot_general | solution.py:60
  1097.5 11.1 fusion.23
  (220 shorter events, 143.9 us)
Async XLA Ops:
  1.8 12.1 %collective-permute-start.2 = (f32[2,2,32,256]{3,2,1,0:T(8,128)S(1)}, f32[2,2,32,256]{3,2,1,0:T(8,128)S(1)}, u32[]{:S(2)}, u32[]{:S(2)}) collective-permute-start(f32[2,2,32,256]{3,2,1,0:T(8,128)S(1)} %get-tuple-element.205), channel_id=1, source_target_pairs={{0,8},{8,16},{16,24},{1,9},{9,17},{17,25},{2,10},{10,18},{18,26},{... | collective-permute-start | bytes 393224 | tf_op jit(solution)/shard_map/ppermute | solution.py:25
  6.6 12.6 %collective-permute-start.3 = (f32[2,2,32,256]{3,2,1,0:T(8,128)S(1)}, f32[2,2,32,256]{3,2,1,0:T(8,128)S(1)}, u32[]{:S(2)}, u32[]{:S(2)}) collective-permute-start(f32[2,2,32,256]{3,2,1,0:T(8,128)S(1)} %get-tuple-element.206), channel_id=1, source_target_pairs={{8,0},{16,8},{24,16},{9,1},{17,9},{25,17},{10,2},{18,10},{26,18},{... | collective-permute-start | bytes 393224 | tf_op jit(solution)/shard_map/ppermute | solution.py:26
  69.4 10.7 collective-permute-start.6
  73.6 7.4 collective-permute-start.7
  74.9 5.0 collective-permute-start.4
  129.3 10.7 collective-permute-start.10
  133.5 7.4 collective-permute-start.11
  134.9 5.0 collective-permute-start.8
  187.1 10.7 collective-permute-start.14
  191.3 7.5 collective-permute-start.15
  192.6 5.0 collective-permute-start.12
  245.7 10.7 collective-permute-start.18
  249.9 7.4 collective-permute-start.19
  251.2 5.0 collective-permute-start.16
  303.4 10.7 collective-permute-start.22
  307.6 7.5 collective-permute-start.23
  309.0 5.0 collective-permute-start.20
  362.2 10.7 collective-permute-start.26
  366.4 7.5 collective-permute-start.27
  367.7 5.1 collective-permute-start.24
  419.6 10.8 collective-permute-start.30
  423.8 7.4 collective-permute-start.31
  425.1 5.3 collective-permute-start.28
  478.4 11.2 %collective-permute-start.34 = (f32[2,2,32,256]{3,2,1,0:T(8,128)S(1)}, f32[2,2,32,256]{3,2,1,0:T(8,128)S(1)}, u32[]{:S(2)}, u32[]{:S(2)}) collective-permute-start(f32[2,2,32,256]{3,2,1,0:T(8,128)S(1)} %get-tuple-element.172), channel_id=1, source_target_pairs={{0,8},{8,16},{16,24},{1,9},{9,17},{17,25},{2,10},{10,18},{18,26},{... | collective-permute-start | bytes 393224 | tf_op jit(solution)/shard_map/ppermute | solution.py:25
  482.6 7.4 collective-permute-start.35
  483.9 5.6 collective-permute-start.32
  535.7 10.7 collective-permute-start.38
  539.9 7.4 collective-permute-start.39
  595.8 14.8 %collective-permute-start.42 = (f32[2,2,32,256]{3,2,1,0:T(8,128)S(1)}, f32[2,2,32,256]{3,2,1,0:T(8,128)S(1)}, u32[]{:S(2)}, u32[]{:S(2)}) collective-permute-start(f32[2,2,32,256]{3,2,1,0:T(8,128)S(1)} %get-tuple-element.164), channel_id=1, source_target_pairs={{0,8},{8,16},{16,24},{1,9},{9,17},{17,25},{2,10},{10,18},{18,26},{... | collective-permute-start | bytes 393224 | tf_op jit(solution)/shard_map/ppermute | solution.py:25
  600.0 10.6 collective-permute-start.43
  601.3 9.3 collective-permute-start.40
  602.6 8.0 collective-permute-start.41
  606.5 357.9 %all-to-all-start = ((f32[8,2,2]{2,1,0:T(2,128)}), f32[8,2,2]{2,1,0:T(2,128)S(1)}, u32[]{:S(2)}, u32[]{:S(2)}) async-start(f32[8,2,2]{2,1,0:T(2,128)} %bitcast.43), calls=%async_computation | async-start | bytes 16384 | tf_op jit(solution)/shard_map/all_to_all | solution.py:124
  657.4 10.7 collective-permute-start.46
  661.6 7.4 collective-permute-start.47
  662.9 5.0 collective-permute-start.44
  716.0 10.7 collective-permute-start.50
  720.2 7.4 collective-permute-start.51
  773.7 10.7 collective-permute-start.54
  777.9 7.4 collective-permute-start.55
  779.2 5.0 collective-permute-start.52
  832.4 10.7 collective-permute-start.58
  836.6 7.4 collective-permute-start.59
  837.9 5.0 collective-permute-start.56
  890.0 10.7 collective-permute-start.62
  894.2 7.4 collective-permute-start.63
  964.4 11.1 %all-to-all-start.1 = ((f32[8,2,2]{1,2,0:T(2,128)}), f32[8,2,2]{1,2,0:T(2,128)S(1)}, u32[]{:S(2)}, u32[]{:S(2)}) async-start(f32[8,2,2]{1,2,0:T(2,128)} %copy.34), calls=%async_computation.1 | async-start | bytes 16384 | tf_op jit(solution)/shard_map/all_to_all | solution.py:123
  975.5 99.2 %all-to-all-start.2 = ((f32[8,2,256,256]{3,2,1,0:T(8,128)}), f32[8,2,256,256]{3,2,1,0:T(8,128)}, u32[]{:S(2)}, u32[]{:S(2)}) async-start(f32[8,2,256,256]{3,2,1,0:T(8,128)} %copy.36), calls=%async_computation.2 | async-start | bytes 8388608 | tf_op jit(solution)/shard_map/all_to_all | solution.py:122
  (26 other events, 841.3 us)
where the time goes:
time: 1120 us; the launch traced here: 1110 us
  blocking collectives  676 us (60%)
  starting transfers between devices  170 us (15%)
  waiting for transfers between devices  109 us (10%)
  other arithmetic  45.2 us (4%)
  between operations  44.9 us (4%)
  matrix products  39.1 us (3%)
  local copies, waits for them, and re-layouts  26 us (2%)
    psum x16, blocking collectives, body(): lax.psum((jnp.sum(velocity * velocity), jnp.sum(push * push)), ('sec', 't...  676 us
    ppermute x32, starting transfers between devices, with_halo(): before = lax.ppermute(last, axis, up)  116 us
    all_to_all x1, waiting for transfers between devices, body(): lax.all_to_all(send_blocks, 'tile', split_axis=0, concat_axis=0, tiled=True)  93.7 us
    ppermute x32, starting transfers between devices, with_halo(): after = lax.ppermute(leading, axis, down)  41.3 us
    reduce_sum x16, other arithmetic, body(): jnp.sum(push * push)  29.4 us
  transfers between devices with their start and end apart: 67, of which 27 were waited for; matrix products, arithmetic and copies ran while one was open for 4% of the time, Pallas kernels for 0%

commit v1 on v0

--- a/solution.py
+++ b/solution.py
@@ -86,7 +86,7 @@
             push = forces(current, refer, coupling, matches, first_sec, sections_all)
             velocity = velocity + delta * push
             speed_sq, push_sq = lax.psum(
-                (jnp.sum(velocity * velocity), jnp.sum(push * push)), ("sec", "tile")
+                lax.psum((jnp.sum(velocity * velocity), jnp.sum(push * push)), "tile"), "sec"
             )
             ratio = jnp.sqrt(speed_sq + EPSILON) / jnp.sqrt(push_sq + EPSILON)
             limit = jnp.minimum(1.0, SPEED_CAP / jnp.sqrt(speed_sq / node_total + EPSILON))

time: 1120 us -> 835 us (0.75)
  blocking collectives: 676 us -> 421 us
  starting transfers between devices: 170 us -> 145 us
    psum x16 -> x32, blocking collectives: 676 us -> 421 us  [the longest x16 235 us: body(): lax.psum((jnp.sum(velocity * velocity), jnp.sum(push * push)), 'tile')]
    ppermute x32, starting transfers between devices: 116 us -> 91.2 us  [with_halo(): before = lax.ppermute(last, axis, up)]
  transfers between devices with their start and end apart: 67 -> 67, of which waited for: 27 -> 27; matrix products, arithmetic and copies ran while one was open for 4% -> 6% of each run, Pallas kernels for 0% -> 0%
where the time goes in v1:
time: 835 us; the launch traced here: 822 us
  blocking collectives  421 us (50%)
  starting transfers between devices  145 us (17%)
  waiting for transfers between devices  101 us (12%)
  other arithmetic  45.4 us (5%)
  between operations  45.3 us (5%)
  matrix products  38.8 us (5%)
  local copies, waits for them, and re-layouts  26.1 us (3%)
    psum x16, blocking collectives, body(): lax.psum((jnp.sum(velocity * velocity), jnp.sum(push * push)), 'tile')  235 us
    psum x16, blocking collectives, body(): lax.psum(lax.psum((jnp.sum(velocity * velocity), jnp.sum(push * push)), '...  185 us
    all_to_all x1, waiting for transfers between devices, body(): lax.all_to_all(send_blocks, 'tile', split_axis=0, concat_axis=0, tiled=True)  93.6 us
    ppermute x32, starting transfers between devices, with_halo(): before = lax.ppermute(last, axis, up)  91.2 us
    ppermute x32, starting transfers between devices, with_halo(): after = lax.ppermute(leading, axis, down)  41.3 us
    reduce_sum x16, other arithmetic, body(): jnp.sum(push * push)  29.6 us
  transfers between devices with their start and end apart: 67, of which 27 were waited for; matrix products, arithmetic and copies ran while one was open for 6% of the time, Pallas kernels for 0%

profile of v1, /device:TPU:0, one launch (start us, length us, event | category | flops | bytes accessed | tf_op | source)
XLA Modules:
  0.0 822.4 jit_solution(4205719594196096988)
XLA Ops:
  1.8 4.9 collective-permute-start.2
  23.0 17.8 %all-reduce.31 = (f32[]{:T(128)}, f32[]{:T(128)}) all-reduce(f32[]{:T(128)} %get-tuple-element.41, f32[]{:T(128)} %get-tuple-element.40), channel_id=1, replica_groups=mesh['sec'=4,'tile'=8] {'tile'}, use_global_device_ids=true, to_apply=%region_1.2 | all-reduce | flops 2 | bytes 16 | tf_op jit(solution)/shard_map/psum | solution.py:89
  40.8 11.7 %all-reduce.47 = (f32[]{:T(128)}, f32[]{:T(128)}) all-reduce(f32[]{:T(128)} %get-tuple-element.76, f32[]{:T(128)} %get-tuple-element.77), channel_id=1, replica_groups=mesh['sec'=4,'tile'=8] {'sec'}, use_global_device_ids=true, to_apply=%region_2.3 | all-reduce | flops 2 | bytes 16 | tf_op jit(solution)/shard_map/psum | solution.py:88
  67.1 14.3 %all-reduce.30 = (f32[]{:T(128)}, f32[]{:T(128)}) all-reduce(f32[]{:T(128)} %get-tuple-element.39, f32[]{:T(128)} %get-tuple-element.38), channel_id=1, replica_groups=mesh['sec'=4,'tile'=8] {'tile'}, use_global_device_ids=true, to_apply=%region_7.8 | all-reduce | flops 2 | bytes 16 | tf_op jit(solution)/shard_map/psum | solution.py:89
  81.3 11.6 %all-reduce.46 = (f32[]{:T(128)}, f32[]{:T(128)}) all-reduce(f32[]{:T(128)} %get-tuple-element.74, f32[]{:T(128)} %get-tuple-element.75), channel_id=1, replica_groups=mesh['sec'=4,'tile'=8] {'sec'}, use_global_device_ids=true, to_apply=%region_8.9 | all-reduce | flops 2 | bytes 16 | tf_op jit(solution)/shard_map/psum | solution.py:88
  101.6 3.0 collective-permute-start.9
  107.6 14.3 %all-reduce.29 = (f32[]{:T(128)}, f32[]{:T(128)}) all-reduce(f32[]{:T(128)} %get-tuple-element.37, f32[]{:T(128)} %get-tuple-element.36), channel_id=1, replica_groups=mesh['sec'=4,'tile'=8] {'tile'}, use_global_device_ids=true, to_apply=%region_13.14 | all-reduce | flops 2 | bytes 16 | tf_op jit(solution)/shard_map/psum | solution.py:89
  121.8 11.6 %all-reduce.45 = (f32[]{:T(128)}, f32[]{:T(128)}) all-reduce(f32[]{:T(128)} %get-tuple-element.72, f32[]{:T(128)} %get-tuple-element.73), channel_id=1, replica_groups=mesh['sec'=4,'tile'=8] {'sec'}, use_global_device_ids=true, to_apply=%region_14.15 | all-reduce | flops 2 | bytes 16 | tf_op jit(solution)/shard_map/psum | solution.py:88
  147.4 14.3 %all-reduce.28 = (f32[]{:T(128)}, f32[]{:T(128)}) all-reduce(f32[]{:T(128)} %get-tuple-element.35, f32[]{:T(128)} %get-tuple-element.34), channel_id=1, replica_groups=mesh['sec'=4,'tile'=8] {'tile'}, use_global_device_ids=true, to_apply=%region_19.20 | all-reduce | flops 2 | bytes 16 | tf_op jit(solution)/shard_map/psum | solution.py:89
  161.7 11.6 %all-reduce.44 = (f32[]{:T(128)}, f32[]{:T(128)}) all-reduce(f32[]{:T(128)} %get-tuple-element.70, f32[]{:T(128)} %get-tuple-element.71), channel_id=1, replica_groups=mesh['sec'=4,'tile'=8] {'sec'}, use_global_device_ids=true, to_apply=%region_20.21 | all-reduce | flops 2 | bytes 16 | tf_op jit(solution)/shard_map/psum | solution.py:88
  181.4 3.0 collective-permute-start.17
  187.2 14.2 %all-reduce.27 = (f32[]{:T(128)}, f32[]{:T(128)}) all-reduce(f32[]{:T(128)} %get-tuple-element.33, f32[]{:T(128)} %get-tuple-element.32), channel_id=1, replica_groups=mesh['sec'=4,'tile'=8] {'tile'}, use_global_device_ids=true, to_apply=%region_25.26 | all-reduce | flops 2 | bytes 16 | tf_op jit(solution)/shard_map/psum | solution.py:89
  201.5 11.6 %all-reduce.43 = (f32[]{:T(128)}, f32[]{:T(128)}) all-reduce(f32[]{:T(128)} %get-tuple-element.68, f32[]{:T(128)} %get-tuple-element.69), channel_id=1, replica_groups=mesh['sec'=4,'tile'=8] {'sec'}, use_global_device_ids=true, to_apply=%region_26.27 | all-reduce | flops 2 | bytes 16 | tf_op jit(solution)/shard_map/psum | solution.py:88
  220.9 3.0 collective-permute-start.21
  226.8 14.3 %all-reduce.26 = (f32[]{:T(128)}, f32[]{:T(128)}) all-reduce(f32[]{:T(128)} %get-tuple-element.31, f32[]{:T(128)} %get-tuple-element.30), channel_id=1, replica_groups=mesh['sec'=4,'tile'=8] {'tile'}, use_global_device_ids=true, to_apply=%region_31.32 | all-reduce | flops 2 | bytes 16 | tf_op jit(solution)/shard_map/psum | solution.py:89
  241.1 11.6 %all-reduce.42 = (f32[]{:T(128)}, f32[]{:T(128)}) all-reduce(f32[]{:T(128)} %get-tuple-element.66, f32[]{:T(128)} %get-tuple-element.67), channel_id=1, replica_groups=mesh['sec'=4,'tile'=8] {'sec'}, use_global_device_ids=true, to_apply=%region_32.33 | all-reduce | flops 2 | bytes 16 | tf_op jit(solution)/shard_map/psum | solution.py:88
  266.6 14.3 %all-reduce.25 = (f32[]{:T(128)}, f32[]{:T(128)}) all-reduce(f32[]{:T(128)} %get-tuple-element.29, f32[]{:T(128)} %get-tuple-element.28), channel_id=1, replica_groups=mesh['sec'=4,'tile'=8] {'tile'}, use_global_device_ids=true, to_apply=%region_37.38 | all-reduce | flops 2 | bytes 16 | tf_op jit(solution)/shard_map/psum | solution.py:89
  280.9 11.6 %all-reduce.41 = (f32[]{:T(128)}, f32[]{:T(128)}) all-reduce(f32[]{:T(128)} %get-tuple-element.64, f32[]{:T(128)} %get-tuple-element.65), channel_id=1, replica_groups=mesh['sec'=4,'tile'=8] {'sec'}, use_global_device_ids=true, to_apply=%region_38.39 | all-reduce | flops 2 | bytes 16 | tf_op jit(solution)/shard_map/psum | solution.py:88
  300.4 3.0 collective-permute-start.29
  306.4 14.3 %all-reduce.24 = (f32[]{:T(128)}, f32[]{:T(128)}) all-reduce(f32[]{:T(128)} %get-tuple-element.27, f32[]{:T(128)} %get-tuple-element.26), channel_id=1, replica_groups=mesh['sec'=4,'tile'=8] {'tile'}, use_global_device_ids=true, to_apply=%region_43.44 | all-reduce | flops 2 | bytes 16 | tf_op jit(solution)/shard_map/psum | solution.py:89
  320.7 11.6 %all-reduce.40 = (f32[]{:T(128)}, f32[]{:T(128)}) all-reduce(f32[]{:T(128)} %get-tuple-element.62, f32[]{:T(128)} %get-tuple-element.63), channel_id=1, replica_groups=mesh['sec'=4,'tile'=8] {'sec'}, use_global_device_ids=true, to_apply=%region_44.45 | all-reduce | flops 2 | bytes 16 | tf_op jit(solution)/shard_map/psum | solution.py:88
  346.1 14.3 %all-reduce.23 = (f32[]{:T(128)}, f32[]{:T(128)}) all-reduce(f32[]{:T(128)} %get-tuple-element.25, f32[]{:T(128)} %get-tuple-element.24), channel_id=1, replica_groups=mesh['sec'=4,'tile'=8] {'tile'}, use_global_device_ids=true, to_apply=%region_49.50 | all-reduce | flops 2 | bytes 16 | tf_op jit(solution)/shard_map/psum | solution.py:89
  360.4 11.6 %all-reduce.39 = (f32[]{:T(128)}, f32[]{:T(128)}) all-reduce(f32[]{:T(128)} %get-tuple-element.60, f32[]{:T(128)} %get-tuple-element.61), channel_id=1, replica_groups=mesh['sec'=4,'tile'=8] {'sec'}, use_global_device_ids=true, to_apply=%region_50.51 | all-reduce | flops 2 | bytes 16 | tf_op jit(solution)/shard_map/psum | solution.py:88
  386.4 14.2 %all-reduce.22 = (f32[]{:T(128)}, f32[]{:T(128)}) all-reduce(f32[]{:T(128)} %get-tuple-element.23, f32[]{:T(128)} %get-tuple-element.22), channel_id=1, replica_groups=mesh['sec'=4,'tile'=8] {'tile'}, use_global_device_ids=true, to_apply=%region_55.56 | all-reduce | flops 2 | bytes 16 | tf_op jit(solution)/shard_map/psum | solution.py:89
  400.6 11.6 %all-reduce.38 = (f32[]{:T(128)}, f32[]{:T(128)}) all-reduce(f32[]{:T(128)} %get-tuple-element.58, f32[]{:T(128)} %get-tuple-element.59), channel_id=1, replica_groups=mesh['sec'=4,'tile'=8] {'sec'}, use_global_device_ids=true, to_apply=%region_56.57 | all-reduce | flops 2 | bytes 16 | tf_op jit(solution)/shard_map/psum | solution.py:88
  424.7 3.5 all-to-all-start
  430.5 17.7 %all-reduce.21 = (f32[]{:T(128)}, f32[]{:T(128)}) all-reduce(f32[]{:T(128)} %get-tuple-element.21, f32[]{:T(128)} %get-tuple-element.20), channel_id=1, replica_groups=mesh['sec'=4,'tile'=8] {'tile'}, use_global_device_ids=true, to_apply=%region_61.62 | all-reduce | flops 2 | bytes 16 | tf_op jit(solution)/shard_map/psum | solution.py:89
  448.2 11.6 %all-reduce.37 = (f32[]{:T(128)}, f32[]{:T(128)}) all-reduce(f32[]{:T(128)} %get-tuple-element.56, f32[]{:T(128)} %get-tuple-element.57), channel_id=1, replica_groups=mesh['sec'=4,'tile'=8] {'sec'}, use_global_device_ids=true, to_apply=%region_62.63 | all-reduce | flops 2 | bytes 16 | tf_op jit(solution)/shard_map/psum | solution.py:88
  473.7 14.3 %all-reduce.20 = (f32[]{:T(128)}, f32[]{:T(128)}) all-reduce(f32[]{:T(128)} %get-tuple-element.19, f32[]{:T(128)} %get-tuple-element.18), channel_id=1, replica_groups=mesh['sec'=4,'tile'=8] {'tile'}, use_global_device_ids=true, to_apply=%region_67.68 | all-reduce | flops 2 | bytes 16 | tf_op jit(solution)/shard_map/psum | solution.py:89
  488.0 11.6 %all-reduce.36 = (f32[]{:T(128)}, f32[]{:T(128)}) all-reduce(f32[]{:T(128)} %get-tuple-element.54, f32[]{:T(128)} %get-tuple-element.55), channel_id=1, replica_groups=mesh['sec'=4,'tile'=8] {'sec'}, use_global_device_ids=true, to_apply=%region_68.69 | all-reduce | flops 2 | bytes 16 | tf_op jit(solution)/shard_map/psum | solution.py:88
  513.6 14.3 %all-reduce.19 = (f32[]{:T(128)}, f32[]{:T(128)}) all-reduce(f32[]{:T(128)} %get-tuple-element.17, f32[]{:T(128)} %get-tuple-element.16), channel_id=1, replica_groups=mesh['sec'=4,'tile'=8] {'tile'}, use_global_device_ids=true, to_apply=%region_73.74 | all-reduce | flops 2 | bytes 16 | tf_op jit(solution)/shard_map/psum | solution.py:89
  527.9 11.6 %all-reduce.35 = (f32[]{:T(128)}, f32[]{:T(128)}) all-reduce(f32[]{:T(128)} %get-tuple-element.52, f32[]{:T(128)} %get-tuple-element.53), channel_id=1, replica_groups=mesh['sec'=4,'tile'=8] {'sec'}, use_global_device_ids=true, to_apply=%region_74.75 | all-reduce | flops 2 | bytes 16 | tf_op jit(solution)/shard_map/psum | solution.py:88
  553.2 14.2 %all-reduce.18 = (f32[]{:T(128)}, f32[]{:T(128)}) all-reduce(f32[]{:T(128)} %get-tuple-element.15, f32[]{:T(128)} %get-tuple-element.14), channel_id=1, replica_groups=mesh['sec'=4,'tile'=8] {'tile'}, use_global_device_ids=true, to_apply=%region_79.80 | all-reduce | flops 2 | bytes 16 | tf_op jit(solution)/shard_map/psum | solution.py:89
  567.5 11.6 %all-reduce.34 = (f32[]{:T(128)}, f32[]{:T(128)}) all-reduce(f32[]{:T(128)} %get-tuple-element.50, f32[]{:T(128)} %get-tuple-element.51), channel_id=1, replica_groups=mesh['sec'=4,'tile'=8] {'sec'}, use_global_device_ids=true, to_apply=%region_80.81 | all-reduce | flops 2 | bytes 16 | tf_op jit(solution)/shard_map/psum | solution.py:88
  592.9 14.3 %all-reduce.17 = (f32[]{:T(128)}, f32[]{:T(128)}) all-reduce(f32[]{:T(128)} %get-tuple-element.13, f32[]{:T(128)} %get-tuple-element.12), channel_id=1, replica_groups=mesh['sec'=4,'tile'=8] {'tile'}, use_global_device_ids=true, to_apply=%region_85.86 | all-reduce | flops 2 | bytes 16 | tf_op jit(solution)/shard_map/psum | solution.py:89
  607.2 11.5 %all-reduce.33 = (f32[]{:T(128)}, f32[]{:T(128)}) all-reduce(f32[]{:T(128)} %get-tuple-element.48, f32[]{:T(128)} %get-tuple-element.49), channel_id=1, replica_groups=mesh['sec'=4,'tile'=8] {'sec'}, use_global_device_ids=true, to_apply=%region_86.87 | all-reduce | flops 2 | bytes 16 | tf_op jit(solution)/shard_map/psum | solution.py:88
  632.5 14.2 %all-reduce.16 = (f32[]{:T(128)}, f32[]{:T(128)}) all-reduce(f32[]{:T(128)} %get-tuple-element.11, f32[]{:T(128)} %get-tuple-element.10), channel_id=1, replica_groups=mesh['sec'=4,'tile'=8] {'tile'}, use_global_device_ids=true, to_apply=%region_91.92 | all-reduce | flops 2 | bytes 16 | tf_op jit(solution)/shard_map/psum | solution.py:89
  646.7 11.5 %all-reduce.32 = (f32[]{:T(128)}, f32[]{:T(128)}) all-reduce(f32[]{:T(128)} %get-tuple-element.46, f32[]{:T(128)} %get-tuple-element.47), channel_id=1, replica_groups=mesh['sec'=4,'tile'=8] {'sec'}, use_global_device_ids=true, to_apply=%region_92.93 | all-reduce | flops 2 | bytes 16 | tf_op jit(solution)/shard_map/psum | solution.py:88
  661.0 8.6 %copy.33 = f32[2,4,32,256]{0,3,2,1:T(8,128)} copy(f32[2,4,32,256]{3,2,1,0:T(8,128)S(1)} %multiply_add_fusion) | data formatting | bytes 524288 | tf_op jit(solution)/shard_map/add | solution.py:95
  669.7 6.3 gather_fusion
  677.1 3.3 all-to-all-start.1
  680.4 4.3 fusion.20
  684.8 3.3 copy.36
  688.0 5.3 all-to-all-start.2
  693.8 93.6 %all-to-all-done.2 = f32[8,2,256,256]{3,2,1,0:T(8,128)} async-done(((f32[8,2,256,256]{3,2,1,0:T(8,128)}), f32[8,2,256,256]{3,2,1,0:T(8,128)}, u32[]{:S(2)}, u32[]{:S(2)}) %all-to-all-start.2) | async-done | bytes 4194336 | tf_op jit(solution)/shard_map/all_to_all | solution.py:122
  787.4 10.3 %fusion.2 = f32[16,256,384]{2,1,0:T(8,128)S(1)} fusion(f32[16,256,256]{2,1,0:T(8,128)} %bitcast.55, f32[16]{0:T(128)S(1)} %sub.591, f32[384,256]{1,0:T(8,128)S(1)} %broadcast_subtract_fusion), kind=kOutput, calls=%fused_computation.3 | convolution fusion | flops 4838129664 | bytes 10879040 | tf_op jit(solution)/shard_map/bij,bkj->bik/dot_general | solution.py:59
  797.7 12.1 %fusion.7 = f32[16,384,384]{2,1,0:T(8,128)S(1)} fusion(f32[16,256,384]{2,1,0:T(8,128)S(1)} %fusion.2, f32[16]{0:T(128)S(1)} %sub.587, f32[384,256]{1,0:T(8,128)S(1)} %broadcast_subtract_fusion), kind=kOutput, calls=%fused_computation.8 | convolution fusion | flops 7254048768 | bytes 16121920 | tf_op jit(solution)/shard_map/bri,bik->brk/dot_general | solution.py:60
  809.7 11.2 %fusion.23 = f32[2,384,384]{2,0,1:T(2,128)S(1)} fusion(f32[8,2,384,384]{3,2,1,0:T(8,128)S(1)} %bitcast.214, f32[8,2,2]{0,2,1:T(2,128)S(1)} %copy.37), kind=kOutput, calls=%fused_computation.24 | convolution fusion | flops 56623104 | bytes 10616960 | tf_op jit(solution)/shard_map/skc,skrq->kcrq/dot_general | solution.py:133
  (236 shorter events, 177.6 us)
Async XLA Ops:
  1.8 12.0 %collective-permute-start.2 = (f32[2,2,32,256]{3,2,1,0:T(8,128)S(1)}, f32[2,2,32,256]{3,2,1,0:T(8,128)S(1)}, u32[]{:S(2)}, u32[]{:S(2)}) collective-permute-start(f32[2,2,32,256]{3,2,1,0:T(8,128)S(1)} %get-tuple-element.237), channel_id=1, source_target_pairs={{0,8},{8,16},{16,24},{1,9},{9,17},{17,25},{2,10},{10,18},{18,26},{... | collective-permute-start | bytes 393224 | tf_op jit(solution)/shard_map/ppermute | solution.py:25
  6.6 12.6 %collective-permute-start.3 = (f32[2,2,32,256]{3,2,1,0:T(8,128)S(1)}, f32[2,2,32,256]{3,2,1,0:T(8,128)S(1)}, u32[]{:S(2)}, u32[]{:S(2)}) collective-permute-start(f32[2,2,32,256]{3,2,1,0:T(8,128)S(1)} %get-tuple-element.238), channel_id=1, source_target_pairs={{8,0},{16,8},{24,16},{9,1},{17,9},{25,17},{10,2},{18,10},{26,18},{... | collective-permute-start | bytes 393224 | tf_op jit(solution)/shard_map/ppermute | solution.py:26
  55.4 8.9 %collective-permute-start.6 = (f32[2,2,32,256]{3,2,1,0:T(8,128)S(1)}, f32[2,2,32,256]{3,2,1,0:T(8,128)S(1)}, u32[]{:S(2)}, u32[]{:S(2)}) collective-permute-start(f32[2,2,32,256]{3,2,1,0:T(8,128)S(1)} %get-tuple-element.232), channel_id=1, source_target_pairs={{0,8},{8,16},{16,24},{1,9},{9,17},{17,25},{2,10},{10,18},{18,26},{... | collective-permute-start | bytes 393224 | tf_op jit(solution)/shard_map/ppermute | solution.py:25
  57.9 6.9 collective-permute-start.7
  59.2 5.0 collective-permute-start.4
  96.4 9.1 %collective-permute-start.10 = (f32[2,2,32,256]{3,2,1,0:T(8,128)S(1)}, f32[2,2,32,256]{3,2,1,0:T(8,128)S(1)}, u32[]{:S(2)}, u32[]{:S(2)}) collective-permute-start(f32[2,2,32,256]{3,2,1,0:T(8,128)S(1)} %get-tuple-element.228), channel_id=1, source_target_pairs={{0,8},{8,16},{16,24},{1,9},{9,17},{17,25},{2,10},{10,18},{18,26},{... | collective-permute-start | bytes 393224 | tf_op jit(solution)/shard_map/ppermute | solution.py:25
  99.0 6.9 collective-permute-start.11
  100.3 5.0 collective-permute-start.8
  136.4 9.0 %collective-permute-start.14 = (f32[2,2,32,256]{3,2,1,0:T(8,128)S(1)}, f32[2,2,32,256]{3,2,1,0:T(8,128)S(1)}, u32[]{:S(2)}, u32[]{:S(2)}) collective-permute-start(f32[2,2,32,256]{3,2,1,0:T(8,128)S(1)} %get-tuple-element.224), channel_id=1, source_target_pairs={{0,8},{8,16},{16,24},{1,9},{9,17},{17,25},{2,10},{10,18},{18,26},{... | collective-permute-start | bytes 393224 | tf_op jit(solution)/shard_map/ppermute | solution.py:25
  138.9 6.9 collective-permute-start.15
  140.2 5.0 collective-permute-start.12
  176.2 9.1 %collective-permute-start.18 = (f32[2,2,32,256]{3,2,1,0:T(8,128)S(1)}, f32[2,2,32,256]{3,2,1,0:T(8,128)S(1)}, u32[]{:S(2)}, u32[]{:S(2)}) collective-permute-start(f32[2,2,32,256]{3,2,1,0:T(8,128)S(1)} %get-tuple-element.220), channel_id=1, source_target_pairs={{0,8},{8,16},{16,24},{1,9},{9,17},{17,25},{2,10},{10,18},{18,26},{... | collective-permute-start | bytes 393224 | tf_op jit(solution)/shard_map/ppermute | solution.py:25
  178.8 6.9 collective-permute-start.19
  180.1 5.0 collective-permute-start.16
  215.7 9.0 %collective-permute-start.22 = (f32[2,2,32,256]{3,2,1,0:T(8,128)S(1)}, f32[2,2,32,256]{3,2,1,0:T(8,128)S(1)}, u32[]{:S(2)}, u32[]{:S(2)}) collective-permute-start(f32[2,2,32,256]{3,2,1,0:T(8,128)S(1)} %get-tuple-element.216), channel_id=1, source_target_pairs={{0,8},{8,16},{16,24},{1,9},{9,17},{17,25},{2,10},{10,18},{18,26},{... | collective-permute-start | bytes 393224 | tf_op jit(solution)/shard_map/ppermute | solution.py:25
  218.2 6.9 collective-permute-start.23
  255.5 9.1 %collective-permute-start.26 = (f32[2,2,32,256]{3,2,1,0:T(8,128)S(1)}, f32[2,2,32,256]{3,2,1,0:T(8,128)S(1)}, u32[]{:S(2)}, u32[]{:S(2)}) collective-permute-start(f32[2,2,32,256]{3,2,1,0:T(8,128)S(1)} %get-tuple-element.212), channel_id=1, source_target_pairs={{0,8},{8,16},{16,24},{1,9},{9,17},{17,25},{2,10},{10,18},{18,26},{... | collective-permute-start | bytes 393224 | tf_op jit(solution)/shard_map/ppermute | solution.py:25
  258.1 6.9 collective-permute-start.27
  259.4 5.1 collective-permute-start.24
  295.3 9.0 %collective-permute-start.30 = (f32[2,2,32,256]{3,2,1,0:T(8,128)S(1)}, f32[2,2,32,256]{3,2,1,0:T(8,128)S(1)}, u32[]{:S(2)}, u32[]{:S(2)}) collective-permute-start(f32[2,2,32,256]{3,2,1,0:T(8,128)S(1)} %get-tuple-element.208), channel_id=1, source_target_pairs={{0,8},{8,16},{16,24},{1,9},{9,17},{17,25},{2,10},{10,18},{18,26},{... | collective-permute-start | bytes 393224 | tf_op jit(solution)/shard_map/ppermute | solution.py:25
  297.8 6.9 collective-permute-start.31
  299.1 5.1 collective-permute-start.28
  334.9 9.6 %collective-permute-start.34 = (f32[2,2,32,256]{3,2,1,0:T(8,128)S(1)}, f32[2,2,32,256]{3,2,1,0:T(8,128)S(1)}, u32[]{:S(2)}, u32[]{:S(2)}) collective-permute-start(f32[2,2,32,256]{3,2,1,0:T(8,128)S(1)} %get-tuple-element.204), channel_id=1, source_target_pairs={{0,8},{8,16},{16,24},{1,9},{9,17},{17,25},{2,10},{10,18},{18,26},{... | collective-permute-start | bytes 393224 | tf_op jit(solution)/shard_map/ppermute | solution.py:25
  337.5 7.0 collective-permute-start.35
  338.8 5.6 collective-permute-start.32
  374.7 9.0 %collective-permute-start.38 = (f32[2,2,32,256]{3,2,1,0:T(8,128)S(1)}, f32[2,2,32,256]{3,2,1,0:T(8,128)S(1)}, u32[]{:S(2)}, u32[]{:S(2)}) collective-permute-start(f32[2,2,32,256]{3,2,1,0:T(8,128)S(1)} %get-tuple-element.200), channel_id=1, source_target_pairs={{0,8},{8,16},{16,24},{1,9},{9,17},{17,25},{2,10},{10,18},{18,26},{... | collective-permute-start | bytes 393224 | tf_op jit(solution)/shard_map/ppermute | solution.py:25
  377.2 6.9 collective-permute-start.39
  378.5 5.0 collective-permute-start.36
  415.6 13.1 %collective-permute-start.42 = (f32[2,2,32,256]{3,2,1,0:T(8,128)S(1)}, f32[2,2,32,256]{3,2,1,0:T(8,128)S(1)}, u32[]{:S(2)}, u32[]{:S(2)}) collective-permute-start(f32[2,2,32,256]{3,2,1,0:T(8,128)S(1)} %get-tuple-element.196), channel_id=1, source_target_pairs={{0,8},{8,16},{16,24},{1,9},{9,17},{17,25},{2,10},{10,18},{18,26},{... | collective-permute-start | bytes 393224 | tf_op jit(solution)/shard_map/ppermute | solution.py:25
  418.2 10.5 %collective-permute-start.43 = (f32[2,2,32,256]{3,2,1,0:T(8,128)S(1)}, f32[2,2,32,256]{3,2,1,0:T(8,128)S(1)}, u32[]{:S(2)}, u32[]{:S(2)}) collective-permute-start(f32[2,2,32,256]{3,2,1,0:T(8,128)S(1)} %get-tuple-element.197), channel_id=1, source_target_pairs={{8,0},{16,8},{24,16},{9,1},{17,9},{25,17},{10,2},{18,10},{26,18},{... | collective-permute-start | bytes 393224 | tf_op jit(solution)/shard_map/ppermute | solution.py:26
  419.5 9.2 %collective-permute-start.40 = (f32[2,4,1,256]{3,2,1,0:T(1,128)S(1)}, f32[2,4,1,256]{3,2,1,0:T(1,128)S(1)}, u32[]{:S(2)}, u32[]{:S(2)}) collective-permute-start(f32[2,4,1,256]{3,2,1,0:T(1,128)S(1)} %get-tuple-element.194), channel_id=1, source_target_pairs={{1,0},{2,1},{3,2},{4,3},{5,4},{6,5},{7,6},{9,8},{10,9},{11,10},{12... | collective-permute-start | bytes 24584 | tf_op jit(solution)/shard_map/ppermute | solution.py:26
  420.8 7.9 collective-permute-start.41
  424.7 252.4 %all-to-all-start = ((f32[8,2,2]{2,1,0:T(2,128)}), f32[8,2,2]{2,1,0:T(2,128)S(1)}, u32[]{:S(2)}, u32[]{:S(2)}) async-start(f32[8,2,2]{2,1,0:T(2,128)} %bitcast.43), calls=%async_computation | async-start | bytes 16384 | tf_op jit(solution)/shard_map/all_to_all | solution.py:124
  462.7 8.9 %collective-permute-start.46 = (f32[2,2,32,256]{3,2,1,0:T(8,128)S(1)}, f32[2,2,32,256]{3,2,1,0:T(8,128)S(1)}, u32[]{:S(2)}, u32[]{:S(2)}) collective-permute-start(f32[2,2,32,256]{3,2,1,0:T(8,128)S(1)} %get-tuple-element.192), channel_id=1, source_target_pairs={{0,8},{8,16},{16,24},{1,9},{9,17},{17,25},{2,10},{10,18},{18,26},{... | collective-permute-start | bytes 393224 | tf_op jit(solution)/shard_map/ppermute | solution.py:25
  465.1 6.9 collective-permute-start.47
  502.4 9.1 %collective-permute-start.50 = (f32[2,2,32,256]{3,2,1,0:T(8,128)S(1)}, f32[2,2,32,256]{3,2,1,0:T(8,128)S(1)}, u32[]{:S(2)}, u32[]{:S(2)}) collective-permute-start(f32[2,2,32,256]{3,2,1,0:T(8,128)S(1)} %get-tuple-element.188), channel_id=1, source_target_pairs={{0,8},{8,16},{16,24},{1,9},{9,17},{17,25},{2,10},{10,18},{18,26},{... | collective-permute-start | bytes 393224 | tf_op jit(solution)/shard_map/ppermute | solution.py:25
  505.0 6.9 collective-permute-start.51
  506.4 5.0 collective-permute-start.48
  542.2 9.0 %collective-permute-start.54 = (f32[2,2,32,256]{3,2,1,0:T(8,128)S(1)}, f32[2,2,32,256]{3,2,1,0:T(8,128)S(1)}, u32[]{:S(2)}, u32[]{:S(2)}) collective-permute-start(f32[2,2,32,256]{3,2,1,0:T(8,128)S(1)} %get-tuple-element.184), channel_id=1, source_target_pairs={{0,8},{8,16},{16,24},{1,9},{9,17},{17,25},{2,10},{10,18},{18,26},{... | collective-permute-start | bytes 393224 | tf_op jit(solution)/shard_map/ppermute | solution.py:25
  544.7 6.9 collective-permute-start.55
  546.0 5.0 collective-permute-start.52
  581.8 9.1 %collective-permute-start.58 = (f32[2,2,32,256]{3,2,1,0:T(8,128)S(1)}, f32[2,2,32,256]{3,2,1,0:T(8,128)S(1)}, u32[]{:S(2)}, u32[]{:S(2)}) collective-permute-start(f32[2,2,32,256]{3,2,1,0:T(8,128)S(1)} %get-tuple-element.180), channel_id=1, source_target_pairs={{0,8},{8,16},{16,24},{1,9},{9,17},{17,25},{2,10},{10,18},{18,26},{... | collective-permute-start | bytes 393224 | tf_op jit(solution)/shard_map/ppermute | solution.py:25
  584.4 6.9 collective-permute-start.59
  621.5 9.0 %collective-permute-start.62 = (f32[2,2,32,256]{3,2,1,0:T(8,128)S(1)}, f32[2,2,32,256]{3,2,1,0:T(8,128)S(1)}, u32[]{:S(2)}, u32[]{:S(2)}) collective-permute-start(f32[2,2,32,256]{3,2,1,0:T(8,128)S(1)} %get-tuple-element.176), channel_id=1, source_target_pairs={{0,8},{8,16},{16,24},{1,9},{9,17},{17,25},{2,10},{10,18},{18,26},{... | collective-permute-start | bytes 393224 | tf_op jit(solution)/shard_map/ppermute | solution.py:25
  623.9 6.9 collective-permute-start.63
  625.3 5.0 collective-permute-start.60
  677.1 10.9 %all-to-all-start.1 = ((f32[8,2,2]{1,2,0:T(2,128)}), f32[8,2,2]{1,2,0:T(2,128)S(1)}, u32[]{:S(2)}, u32[]{:S(2)}) async-start(f32[8,2,2]{1,2,0:T(2,128)} %copy.34), calls=%async_computation.1 | async-start | bytes 16384 | tf_op jit(solution)/shard_map/all_to_all | solution.py:123
  688.0 99.3 %all-to-all-start.2 = ((f32[8,2,256,256]{3,2,1,0:T(8,128)}), f32[8,2,256,256]{3,2,1,0:T(8,128)}, u32[]{:S(2)}, u32[]{:S(2)}) async-start(f32[8,2,256,256]{3,2,1,0:T(8,128)} %copy.36), calls=%async_computation.2 | async-start | bytes 8388608 | tf_op jit(solution)/shard_map/all_to_all | solution.py:122
  (26 other events, 631.0 us)
